TPU v7x, 128 devices: a whole 4x4x4 slice. The times are simulated.
128 devices in a mesh: tok: 16 (over x, z), head: 8 (over y, core).
Axes of the slice: x: 4, y: 4, z: 4, core: 2. Of those that a mesh axis runs over, the one named last changes fastest.
Arguments:
- tokens: bfloat16 [4096, 2880], P(('tok', 'head')), may hold values from -6 to 6
- lengths: int32 [4], replicated, may hold values from 1 to 2048, 3968 in all
- norm_gain_attn: float32 [2880], replicated, may hold values from 0.1 to 1.9
- query_key_value_weight: bfloat16 [2880, 5120], P(None, 'head'), may hold values from -0.109375 to 0.109375
- sinks: float32 [64], P('head'), may hold values from 1 to 6
- w_out_attn: bfloat16 [4096, 2880], P('head'), may hold values from -0.09375 to 0.09375
- norm_gain_moe: float32 [2880], replicated, may hold values from 0.1 to 1.9
- routes: int32 [4096, 4], P(('tok', 'head')), may hold values from 0 to 31, all different within a row; in each aligned block of 32 rows (0 to 31, 32 to 63, ...) at most 6 rows name the same one
- gates: float32 [4096, 4], P(('tok', 'head')), may hold values from 0.1 to 1
- w_in: bfloat16 [128, 2880, 1440], P(('tok', 'head')), may hold values from -0.109375 to 0.109375
- w_down: bfloat16 [128, 720, 2880], P(('tok', 'head')), may hold values from -0.109375 to 0.109375
- page_table: int32 [256], replicated, may hold values from 0 to 255, as said below
Outputs:
- hidden_out: bfloat16 [4096, 2880], P(('tok', 'head'))
- kv_cache: bfloat16 [8, 256, 16, 128], P('head', 'tok')
Inputs may be any that keep to these rules, and one draw needn't show every extreme that they name: `routes`: every row names 4 different experts. In each aligned block of 32 rows no expert is named by more than 6 rows, and in every draw some block has an expert named by exactly 6 rows. `lengths`: they sum to 3968, and the longest is exactly 2048. `page_table`: A permutation. Of the 16 logical pages in each aligned block of 16, exactly 1 map into each aligned block of 16 physical pages.
All inputs are finite; a program needn't handle non-finite values.
Results may differ from a plain program's by a relative error of at most 0.018.
Values may be sent and summed in bfloat16 or wider, within the bound.
A program may use at most 128 MiB of HBM per device.

v0:
```python
import math
import jax
import jax.numpy as jnp
from jax import lax
from jax.sharding import PartitionSpec as P

MODEL_WIDTH = 2880
HEAD_SIZE = 64
EXPERTS = 32
ATTEND_WINDOW = 128
NSEQ = 4
PAGE_TOKENS = 16
QUERY_PER_KEY = 8
EPSILON = 1e-05
ROPE_BASE = 150000.0
GLU_ALPHA = 1.702


def passed_along(array, axis, by):
    peers = lax.axis_size(axis)
    pairs = [(i, i + by) for i in range(peers) if 0 <= i + by < peers]
    return lax.ppermute(array, axis, pairs)


def normalize(values, gain_vec):
    wide = values.astype(jnp.float32)
    inv_rms = lax.rsqrt(jnp.mean(wide * wide, axis=-1, keepdims=True) + EPSILON)
    return wide * inv_rms * gain_vec


def segment_table(lengths, row_index):
    seq_ends = jnp.cumsum(lengths)
    starts = jnp.concatenate([jnp.zeros((1,), jnp.int32), seq_ends])
    segment = jnp.sum((row_index[:, None] >= seq_ends[None, :]).astype(jnp.int32), axis=1)
    onehot = segment[:, None] == jnp.arange(starts.shape[0], dtype=jnp.int32)[None, :]
    seg_start = jnp.sum(jnp.where(onehot, starts[None, :], 0), axis=1)
    return (segment, row_index - seg_start)


def rotate(values, positions):
    half_dim = values.shape[-1] // 2
    inv_freq = jnp.exp(
        jnp.arange(half_dim, dtype=jnp.float32) * (-2.0 * math.log(ROPE_BASE) / values.shape[-1])
    )
    angles = positions.astype(jnp.float32)[:, None] * inv_freq[None, :]
    view_shape = (angles.shape[0],) + (1,) * (values.ndim - 2) + (half_dim,)
    cos_table = jnp.cos(angles).reshape(view_shape)
    sin_table = jnp.sin(angles).reshape(view_shape)
    lower_half = values[..., :half_dim]
    upper_half = values[..., half_dim:]
    return jnp.concatenate(
        [
            lower_half * cos_table - upper_half * sin_table,
            upper_half * cos_table + lower_half * sin_table,
        ],
        axis=-1,
    )


def band_mask(query_index, key_index, query_segs, key_segs, window):
    nblocks = query_index.shape[0] // window
    query_pos = query_index.reshape(nblocks, window)
    query_seg = query_segs.reshape(nblocks, window)
    key_grid = key_index.reshape(nblocks + 1, window)
    seg_grid = key_segs.reshape(nblocks + 1, window)
    key_pos = jnp.concatenate([key_grid[:-1], key_grid[1:]], axis=1)
    key_seg = jnp.concatenate([seg_grid[:-1], seg_grid[1:]], axis=1)
    distance = query_pos[:, :, None] - key_pos[:, None, :]
    allowed = (query_seg[:, :, None] == key_seg[:, None, :]) & (query_seg < NSEQ)[:, :, None]
    allowed = allowed & (key_pos >= 0)[:, None, :] & (distance >= 0) & (distance < window)
    return allowed


def band_attention(query_rows, extended, sink_table, allowed):
    nblocks = allowed.shape[0]
    groups = sink_table.shape[0]
    query_blocks = query_rows.reshape(nblocks, ATTEND_WINDOW, groups, QUERY_PER_KEY, HEAD_SIZE)
    pair_grid = extended.reshape(nblocks + 1, ATTEND_WINDOW, groups, 2 * HEAD_SIZE)
    key_band = jnp.concatenate([pair_grid[:-1], pair_grid[1:]], axis=1)
    scores = jnp.einsum(
        "bqgnh,bkgh->bgnqk",
        query_blocks,
        key_band[..., :HEAD_SIZE],
        preferred_element_type=jnp.float32,
    )
    weights = jnp.where(allowed[:, None, None], jnp.exp(scores), 0.0)
    totals = jnp.sum(weights, axis=-1, keepdims=True) + jnp.exp(sink_table)[None, :, :, None, None]
    probs_bf = (weights / totals).astype(jnp.bfloat16)
    outputs = jnp.einsum(
        "bgnqk,bkgh->bqgnh", probs_bf, key_band[..., HEAD_SIZE:], preferred_element_type=jnp.float32
    )
    return outputs.astype(jnp.bfloat16).reshape(
        nblocks * ATTEND_WINDOW, groups * QUERY_PER_KEY * HEAD_SIZE
    )


def expert_mlp(rows_in, w_in_local, w_down_local):
    ffs_local = w_down_local.shape[0]
    gate_up = jnp.dot(rows_in, w_in_local, preferred_element_type=jnp.float32)
    gate_part = gate_up[:, :ffs_local]
    up_part = gate_up[:, ffs_local:]
    activated = ((up_part + 1.0) * gate_part * jax.nn.sigmoid(GLU_ALPHA * gate_part)).astype(
        jnp.bfloat16
    )
    return jnp.dot(activated, w_down_local, preferred_element_type=jnp.float32).astype(jnp.bfloat16)


def copied_route(outgoing, route, width_split, slots, w_in_local, w_down_local):
    spread = jnp.broadcast_to(
        outgoing[:, None], (EXPERTS, width_split, slots, MODEL_WIDTH)
    ).reshape(EXPERTS * width_split, slots, MODEL_WIDTH)
    incoming = route(spread)
    produced = expert_mlp(incoming.reshape(-1, MODEL_WIDTH), w_in_local, w_down_local).reshape(
        spread.shape
    )
    returned = route(produced)
    return jnp.sum(
        returned.astype(jnp.float32).reshape(EXPERTS, width_split, slots, MODEL_WIDTH), axis=1
    ).reshape(EXPERTS * slots, MODEL_WIDTH)


def page_order(page_table, n_tok, pages_dev):
    page_grid = page_table.reshape(n_tok, pages_dev)
    target = page_grid // pages_dev
    page_ids = jnp.arange(pages_dev, dtype=jnp.int32)
    earlier = page_ids[:, None] > page_ids[None, :]
    same_dest = target[:, :, None] == target[:, None, :]
    order_rank = jnp.sum((same_dest & earlier[None]).astype(jnp.int32), axis=2)
    return (target, order_rank, page_grid % pages_dev)


def per_device(
    tokens,
    lengths,
    norm_gain_attn,
    query_key_value_weight,
    sinks,
    w_out_attn,
    norm_gain_moe,
    routes,
    gates,
    w_in,
    w_down,
    page_table,
):
    n_tok = lax.axis_size("tok")
    n_head = lax.axis_size("head")
    tok_id = lax.axis_index("tok")
    head_id = lax.axis_index("head")
    row_count = tokens.shape[0]
    tok_dev = row_count * n_head
    groups = sinks.shape[0] // QUERY_PER_KEY
    normed_input = normalize(tokens, norm_gain_attn).astype(jnp.bfloat16)
    projected_rows = jnp.dot(
        lax.all_gather(normed_input, "head", axis=0, tiled=True),
        query_key_value_weight,
        preferred_element_type=jnp.float32,
    ).reshape(tok_dev, groups, QUERY_PER_KEY + 2, HEAD_SIZE)
    row_base = tok_id * tok_dev
    query_index = row_base + jnp.arange(tok_dev, dtype=jnp.int32)
    query_segs, positions = segment_table(lengths, query_index)
    query_rows = (
        rotate(projected_rows[:, :, :QUERY_PER_KEY], positions) * HEAD_SIZE ** (-0.5)
    ).astype(jnp.bfloat16)
    key_rot = rotate(projected_rows[:, :, QUERY_PER_KEY], positions)
    key_value_pairs = jnp.concatenate(
        [key_rot, projected_rows[:, :, QUERY_PER_KEY + 1]], axis=-1
    ).astype(jnp.bfloat16)
    rim_rows = passed_along(key_value_pairs[tok_dev - ATTEND_WINDOW :], "tok", 1)
    key_index = row_base - ATTEND_WINDOW + jnp.arange(tok_dev + ATTEND_WINDOW, dtype=jnp.int32)
    key_segs, _ = segment_table(lengths, key_index)
    allowed = band_mask(query_index, key_index, query_segs, key_segs, ATTEND_WINDOW)
    attended = band_attention(
        query_rows,
        jnp.concatenate([rim_rows, key_value_pairs], axis=0),
        sinks.reshape(groups, QUERY_PER_KEY),
        allowed,
    )
    attn_sum = lax.psum_scatter(
        jnp.dot(attended, w_out_attn, preferred_element_type=jnp.float32).astype(jnp.bfloat16),
        "head",
        scatter_dimension=0,
        tiled=True,
    ).astype(jnp.float32)
    resid = tokens.astype(jnp.float32) + attn_sum
    moe_in = normalize(resid, norm_gain_moe).astype(jnp.bfloat16)
    own_index = row_base + head_id * row_count + jnp.arange(row_count, dtype=jnp.int32)
    own_segs, _ = segment_table(lengths, own_index)
    is_live = own_segs < NSEQ
    capacity = row_count // 8 + 2
    width_split = n_tok * n_head // EXPERTS
    expert_ids = jnp.arange(EXPERTS, dtype=jnp.int32)
    naming = routes[:, :, None] == expert_ids[None, None, :]
    routed = (jnp.any(naming, axis=1) & is_live[:, None]).astype(jnp.int32)
    slot_rank = jnp.cumsum(routed, axis=0) - 1
    slot_ids = jnp.arange(capacity, dtype=jnp.int32)
    placed = (routed == 1)[:, :, None] & (slot_rank[:, :, None] == slot_ids[None, None, :])
    local_ids = jnp.arange(row_count, dtype=jnp.int32)
    source_row = jnp.sum(jnp.where(placed, local_ids[:, None, None], 0), axis=0)
    filled = jnp.any(placed, axis=0)
    outgoing = jnp.where(filled[:, :, None], moe_in[source_row], jnp.zeros((), jnp.bfloat16))

    def flat_route(blocks):
        return lax.all_to_all(blocks, ("tok", "head"), split_axis=0, concat_axis=0, tiled=True)

    summed = copied_route(outgoing, flat_route, width_split, capacity, w_in[0], w_down[0])
    chosen_rank = jnp.sum(jnp.where(naming, slot_rank[:, None, :], 0), axis=2)
    pick_rows = routes * capacity + jnp.clip(chosen_rank, 0, capacity - 1)
    weighted = jnp.where(is_live[:, None], gates, 0.0)
    expert_sum = jnp.sum(summed[pick_rows] * weighted[:, :, None], axis=1)
    hidden_out = (resid + expert_sum).astype(jnp.bfloat16)
    pages_dev = tok_dev // PAGE_TOKENS
    share_count = pages_dev // n_tok
    paged = key_value_pairs.reshape(pages_dev, PAGE_TOKENS, groups, 2 * HEAD_SIZE)
    target, order_rank, slot_grid = page_order(page_table, n_tok, pages_dev)
    dest_ids = jnp.arange(n_tok, dtype=jnp.int32)
    share_ids = jnp.arange(share_count, dtype=jnp.int32)
    page_ids = jnp.arange(pages_dev, dtype=jnp.int32)
    my_target = target[tok_id]
    my_rank = order_rank[tok_id]
    matched = (my_target[:, None, None] == dest_ids[None, :, None]) & (
        my_rank[:, None, None] == share_ids[None, None, :]
    )
    pick_page = jnp.sum(jnp.where(matched, page_ids[:, None, None], 0), axis=0)
    arrived = lax.all_to_all(paged[pick_page], "tok", split_axis=0, concat_axis=0, tiled=True)
    to_here = (target == tok_id)[:, :, None] & (order_rank[:, :, None] == share_ids[None, None, :])
    landing = jnp.sum(jnp.where(to_here, slot_grid[:, :, None], 0), axis=1)
    stored = jnp.zeros_like(paged).at[landing.reshape(-1)].set(arrived.reshape(paged.shape))
    kv_cache = jnp.transpose(stored, (2, 0, 1, 3))
    return (hidden_out, kv_cache)


def solution(mesh):
    return jax.shard_map(
        per_device,
        mesh=mesh,
        in_specs=(
            P(("tok", "head"), None),
            P(),
            P(),
            P(None, "head"),
            P("head"),
            P("head", None),
            P(),
            P(("tok", "head"), None),
            P(("tok", "head"), None),
            P(("tok", "head"), None, None),
            P(("tok", "head"), None, None),
            P(),
        ),
        out_specs=(P(("tok", "head"), None), P("head", "tok", None, None)),
        check_vma=False,
    )
```

profile of v0, /device:TPU:0, one launch (start us, length us, event | category | flops | bytes accessed | tf_op | source)
XLA Modules:
  0.0 337.7 jit_solution(5325949729311232361)
XLA Ops:
  7.2 1.2 fusion.13
  8.5 1.7 fusion.15
  10.3 1.2 exp.30
  11.5 0.8 reduce-window.8
  12.9 0.8 multiply_cosine_fusion
  13.7 0.9 fusion.22
  14.6 22.5 %all-gather.2.cloned.1.call-done = bf16[256,2880]{1,0:T(8,128)(2,1)} async-done(((bf16[32,2880]{1,0:T(8,128)(2,1)}), bf16[256,2880]{1,0:T(8,128)(2,1)}) %all-gather.2.cloned.1.call-update) | async-done | bytes 1474576 | tf_op jit(solution)/shard_map/all_gather | solution.py:155
  37.1 4.1 %fusion.49 = f32[256,640]{0,1:T(8,128)S(1)} fusion(bf16[256,2880]{1,0:T(8,128)(2,1)} %all-gather.2.cloned.1.call-done, bf16[2880,640]{1,0:T(8,128)(2,1)} %param.15), kind=kOutput, calls=%fused_computation.145 | convolution fusion | flops 943718400 | bytes 5816320 | tf_op jit(solution)/shard_map/dot_general | solution.py:154
  41.4 0.6 pad_maximum_fusion.3
  42.0 4.1 %collective-permute-start = (bf16[128,1,128]{0,2,1:T(8,128)(2,1)}, bf16[128,1,128]{0,2,1:T(8,128)(2,1)}, u32[]{:S(2)}, u32[]{:S(2)}) collective-permute-start(bf16[128,1,128]{0,2,1:T(8,128)(2,1)} %pad_maximum_fusion.3), channel_id=1, source_target_pairs={{0,8},{8,16},{16,24},{24,32},{32,40},{40,48},{48,56},{56,64},{64,7... | collective-permute-start | bytes 98312 | tf_op jit(solution)/shard_map/ppermute | solution.py:22
  46.2 0.6 copy_bitcast_fusion
  46.8 0.6 slice.143
  47.4 1.4 concatenate.80
  48.8 1.4 copy.75
  50.1 0.8 concatenate.85
  51.0 1.7 copy.77
  52.8 0.8 pad_maximum_fusion
  53.9 0.8 maximum_maximum_fusion
  54.7 1.5 fusion.6
  56.2 0.5 fusion.7
  56.8 0.3 copy.80
  57.1 2.2 convolution_convert_fusion.1
  60.1 31.5 %reduce-scatter.2.cloned.1.call-done = bf16[32,2880]{1,0:T(8,128)(2,1)} async-done(((bf16[256,2880]{1,0:T(8,128)(2,1)}), bf16[32,2880]{1,0:T(8,128)(2,1)}) %reduce-scatter.2.cloned.1.call-update) | async-done | bytes 184336 | tf_op jit(solution)/shard_map/reduce_scatter | solution.py:179
  91.6 1.1 multiply_reduce_fusion.1
  92.7 1.0 multiply_convert_fusion
  93.7 1.3 gather_fusion
  95.1 1.4 reshape.832
  96.5 1.6 broadcast_select_fusion
  98.1 3.0 broadcast_in_dim.93
  101.1 8.1 %all-to-all-start = ((bf16[128,6,2880]{2,1,0:T(8,128)(2,1)}), bf16[128,6,2880]{2,1,0:T(8,128)(2,1)}, u32[]{:S(2)}, u32[]{:S(2)}) async-start(bf16[128,6,2880]{2,1,0:T(8,128)(2,1)} %bitcast.119), calls=%async_computation.1 | async-start | bytes 12058624 | tf_op jit(solution)/shard_map/all_to_all | solution.py:204
  109.3 0.4 convert_reduce_fusion.1
  110.4 1.2 gather_fusion.2
  111.6 70.6 %all-to-all-done = bf16[128,6,2880]{2,1,0:T(8,128)(2,1)} async-done(((bf16[128,6,2880]{2,1,0:T(8,128)(2,1)}), bf16[128,6,2880]{2,1,0:T(8,128)(2,1)}, u32[]{:S(2)}, u32[]{:S(2)}) %all-to-all-start) | async-done | bytes 4423712 | tf_op jit(solution)/shard_map/all_to_all | solution.py:204
  182.2 6.4 %all-to-all-start.2 = ((bf16[16,1,16,1,128]{4,2,3,1,0:T(8,128)(2,1)}), bf16[16,1,16,1,128]{4,2,3,1,0:T(8,128)(2,1)S(1)}, u32[]{:S(2)}, u32[]{:S(2)}) async-start(bf16[16,1,16,1,128]{4,2,3,1,0:T(8,128)(2,1)} %bitcast.37), calls=%async_computation.3 | async-start | bytes 131072 | tf_op jit(solution)/shard_map/all_to_all | solution.py:225
  188.6 8.2 %reshape.821 = bf16[768,2880]{1,0:T(8,128)(2,1)} reshape(bf16[128,6,2880]{2,1,0:T(8,128)(2,1)} %all-to-all-done) | data formatting | bytes 8847360 | tf_op jit(solution)/shard_map/reshape | solution.py:113
  196.8 10.8 %fusion = f32[768,1440]{0,1:T(8,128)S(1)} fusion(bf16[768,2880]{1,0:T(8,128)(2,1)} %reshape.821, bf16[1,2880,1440]{1,2,0:T(8,128)(2,1)} %param.21), kind=kOutput, calls=%fused_computation.5 | convolution fusion | flops 6370099200 | bytes 17141760 | tf_op jit(solution)/shard_map/dot_general | solution.py:99
  207.6 8.1 %convolution_convert_fusion = bf16[768,2880]{0,1:T(8,128)(2,1)} fusion(bf16[1,720,2880]{2,1,0:T(8,128)(2,1)} %param.22, f32[768,1440]{0,1:T(8,128)S(1)} %fusion), kind=kOutput, calls=%fused_computation.7 | convolution fusion | flops 3191685120 | bytes 12994560 | tf_op jit(solution)/shard_map/dot_general | solution.py:105
  215.7 6.5 %copy.83 = bf16[768,2880]{1,0:T(8,128)(2,1)} copy(bf16[768,2880]{0,1:T(8,128)(2,1)} %convolution_convert_fusion) | data formatting | bytes 8847360 | tf_op jit(solution)/shard_map/convert_element_type | solution.py:105
  222.2 7.6 %reshape.822 = bf16[128,6,2880]{2,1,0:T(8,128)(2,1)} reshape(bf16[768,2880]{1,0:T(8,128)(2,1)} %copy.83) | data formatting | bytes 8847360 | tf_op jit(solution)/shard_map/reshape | solution.py:113
  229.8 8.6 %all-to-all-start.1 = ((bf16[128,6,2880]{2,1,0:T(8,128)(2,1)}), bf16[128,6,2880]{2,1,0:T(8,128)(2,1)}, u32[]{:S(2)}, u32[]{:S(2)}) async-start(bf16[128,6,2880]{2,1,0:T(8,128)(2,1)} %reshape.822), calls=%async_computation.2 | async-start | bytes 12058624 | tf_op jit(solution)/shard_map/all_to_all | solution.py:204
  239.2 1.0 scatter_fusion
  240.2 71.0 %all-to-all-done.1 = bf16[128,6,2880]{2,1,0:T(8,128)(2,1)} async-done(((bf16[128,6,2880]{2,1,0:T(8,128)(2,1)}), bf16[128,6,2880]{2,1,0:T(8,128)(2,1)}, u32[]{:S(2)}, u32[]{:S(2)}) %all-to-all-start.1) | async-done | bytes 4423712 | tf_op jit(solution)/shard_map/all_to_all | solution.py:204
  311.2 6.0 %convert_reduce_fusion = f32[32,6,2880]{2,1,0:T(8,128)} fusion(bf16[128,6,2880]{2,1,0:T(8,128)(2,1)} %all-to-all-done.1), kind=kLoop, calls=%fused_computation.4 | loop fusion | flops 3870720 | bytes 6635520 | tf_op jit(solution)/shard_map/reduce_sum | solution.py:117
  317.2 3.0 reshape.825
  320.2 4.6 %gather_fusion.1 = f32[128,2880]{1,0:T(8,128)} fusion(f32[192,2880]{1,0:T(8,128)} %reshape.825, s32[1024]{0:T(1024)S(1)} %pad_clamp_fusion.1), kind=kCustom, calls=%fused_computation.1 | custom fusion | bytes 2949632 | tf_op jit(solution)/shard_map/gather | solution.py:210
  324.9 2.8 reshape.840
  327.7 2.4 multiply_reduce_fusion
  330.1 0.7 add_convert_fusion
  (101 shorter events, 3.6 us)
Async XLA Ops:
  7.2 49.9 %copy-start = (bf16[512,2880]{0,1:T(8,128)(2,1)S(1)}, bf16[512,2880]{0,1:T(8,128)(2,1)}, u32[]{:S(2)}) copy-start(bf16[512,2880]{0,1:T(8,128)(2,1)} %param.17) | copy-start | bytes 8847364
  7.2 29.9 %all-gather.2.cloned.1.call-start = ((), (), s32[]{:S(2)}) async-start(), calls=%async_computation.4 | async-start | bytes 1695744 | tf_op jit(solution)/shard_map/all_gather | solution.py:155
  10.2 81.4 %reduce-scatter.2.cloned.1.call-start = ((), (), s32[]{:S(2)}) async-start(), calls=%async_computation.5 | async-start | bytes 1695744 | tf_op jit(solution)/shard_map/reduce_scatter | solution.py:179
  12.3 0.5 copy-start.12
  37.1 9.0 %copy-start.7 = (f32[256,32]{0,1:T(8,128)S(1)}, f32[256,32]{0,1:T(8,128)}, u32[]{:S(2)}) copy-start(f32[256,32]{0,1:T(8,128)} %get-tuple-element.12) | copy-start | bytes 98308
  37.1 9.0 %copy-start.8 = (f32[256,32]{0,1:T(8,128)S(1)}, f32[256,32]{0,1:T(8,128)}, u32[]{:S(2)}) copy-start(f32[256,32]{0,1:T(8,128)} %get-tuple-element.13) | copy-start | bytes 98308
  42.0 10.8 %collective-permute-start = (bf16[128,1,128]{0,2,1:T(8,128)(2,1)}, bf16[128,1,128]{0,2,1:T(8,128)(2,1)}, u32[]{:S(2)}, u32[]{:S(2)}) collective-permute-start(bf16[128,1,128]{0,2,1:T(8,128)(2,1)} %pad_maximum_fusion.3), channel_id=1, source_target_pairs={{0,8},{8,16},{16,24},{24,32},{32,40},{40,48},{48,56},{56,64},{64,7... | collective-permute-start | bytes 98312 | tf_op jit(solution)/shard_map/ppermute | solution.py:22
  52.8 3.4 %copy-start.5 = (pred[2,128,256]{1,2,0:T(8,128)(4,1)S(1)}, pred[2,128,256]{1,2,0:T(8,128)(4,1)}, u32[]{:S(2)}) copy-start(pred[2,128,256]{1,2,0:T(8,128)(4,1)} %fusion.22) | copy-start | bytes 196612
  53.6 2.5 copy-start.15
  57.0 2.3 copy-start.13
  57.1 2.4 copy-start.9
  57.1 34.5 %copy-start.2 = (bf16[32,2880]{1,0:T(8,128)(2,1)S(1)}, bf16[32,2880]{1,0:T(8,128)(2,1)}, u32[]{:S(2)}) copy-start(bf16[32,2880]{1,0:T(8,128)(2,1)} %param.12) | copy-start | bytes 552964
  57.1 35.6 %copy-start.10 = (f32[2880]{0:T(1024)S(1)}, f32[2880]{0:T(1024)}, u32[]{:S(2)}) copy-start(f32[2880]{0:T(1024)} %param.18) | copy-start | bytes 34564
  101.1 8.1 %copy-start.11 = (s32[256]{0:T(256)S(1)}, s32[256]{0:T(256)}, u32[]{:S(2)}) copy-start(s32[256]{0:T(256)} %param.23) | copy-start | bytes 3076
  101.1 9.0 %copy-start.4 = (bf16[256,1,1,64]{0,3,2,1:T(8,128)(2,1)S(1)}, bf16[256,1,1,64]{0,3,2,1:T(8,128)(2,1)}, u32[]{:S(2)}) copy-start(bf16[256,1,1,64]{0,3,2,1:T(8,128)(2,1)} %slice.143) | copy-start | bytes 98308
  101.1 81.1 %all-to-all-start = ((bf16[128,6,2880]{2,1,0:T(8,128)(2,1)}), bf16[128,6,2880]{2,1,0:T(8,128)(2,1)}, u32[]{:S(2)}, u32[]{:S(2)}) async-start(bf16[128,6,2880]{2,1,0:T(8,128)(2,1)} %bitcast.119), calls=%async_computation.1 | async-start | bytes 12058624 | tf_op jit(solution)/shard_map/all_to_all | solution.py:204
  182.2 47.6 %all-to-all-start.2 = ((bf16[16,1,16,1,128]{4,2,3,1,0:T(8,128)(2,1)}), bf16[16,1,16,1,128]{4,2,3,1,0:T(8,128)(2,1)S(1)}, u32[]{:S(2)}, u32[]{:S(2)}) async-start(bf16[16,1,16,1,128]{4,2,3,1,0:T(8,128)(2,1)} %bitcast.37), calls=%async_computation.3 | async-start | bytes 131072 | tf_op jit(solution)/shard_map/all_to_all | solution.py:225
  229.8 9.1 %copy-start.14 = (f32[32,4]{0,1:T(4,128)S(1)}, f32[32,4]{0,1:T(4,128)}, u32[]{:S(2)}) copy-start(f32[32,4]{0,1:T(4,128)} %param.20) | copy-start | bytes 1540
  229.8 81.4 %all-to-all-start.1 = ((bf16[128,6,2880]{2,1,0:T(8,128)(2,1)}), bf16[128,6,2880]{2,1,0:T(8,128)(2,1)}, u32[]{:S(2)}, u32[]{:S(2)}) async-start(bf16[128,6,2880]{2,1,0:T(8,128)(2,1)} %reshape.822), calls=%async_computation.2 | async-start | bytes 12058624 | tf_op jit(solution)/shard_map/all_to_all | solution.py:204
  240.2 77.0 %copy-start.6 = (bf16[16,16,128]{2,1,0:T(8,128)(2,1)}, bf16[16,16,128]{2,1,0:T(8,128)(2,1)S(1)}, u32[]{:S(2)}) copy-start(bf16[16,16,128]{2,1,0:T(8,128)(2,1)S(1)} %scatter_fusion) | copy-start | bytes 196612
  320.2 10.6 %copy-start.1 = (bf16[512,2880]{0,1:T(8,128)(2,1)S(1)}, bf16[512,2880]{0,1:T(8,128)(2,1)}, u32[]{:S(2)}) copy-start(bf16[512,2880]{0,1:T(8,128)(2,1)} %param.17) | copy-start | bytes 8847364
  324.9 5.2 %copy-start.3 = (bf16[32,2880]{1,0:T(8,128)(2,1)S(1)}, bf16[32,2880]{1,0:T(8,128)(2,1)}, u32[]{:S(2)}) copy-start(bf16[32,2880]{1,0:T(8,128)(2,1)} %reduce-scatter.2.cloned.1.call-done) | copy-start | bytes 552964
Sparse Core Ops, SparseCore 0:
  10.3 26.7 all-gather.1
  59.4 32.1 reduce-scatter.1
where the time goes:
time: 339 us; the launch traced here: 338 us
  waiting for transfers between devices  196 us (58%)
  local copies, waits for them, and re-layouts  50.4 us (15%)
  starting transfers between devices  27.2 us (8%)
  matrix products  27.2 us (8%)
  other arithmetic  22.7 us (7%)
  between operations  14.5 us (4%)
    all_to_all x2, waiting for transfers between devices, flat_route(): lax.all_to_all(blocks, ('tok', 'head'), split_axis=0, concat_axis=0, tile...  142 us
    reduce_scatter x1, waiting for transfers between devices, per_device(): lax.psum_scatter(jnp.dot(attended, w_out_attn, preferred_element_type=jnp...  31.5 us
    all_gather x1, waiting for transfers between devices, per_device(): lax.all_gather(normed_input, 'head', axis=0, tiled=True)  22.5 us
    all_to_all x2, starting transfers between devices, flat_route(): lax.all_to_all(blocks, ('tok', 'head'), split_axis=0, concat_axis=0, tile...  16.7 us
    dot_general x1, matrix products, expert_mlp(): gate_up = jnp.dot(rows_in, w_in_local, preferred_element_type=jnp.float32)  10.8 us
    reshape x1, local copies, waits for them, and re-layouts, copied_route(): incoming.reshape(-1, MODEL_WIDTH)  8.19 us
    dot_general x1, matrix products, expert_mlp(): jnp.dot(activated, w_down_local, preferred_element_type=jnp.float32)  8.09 us
    reshape x1, local copies, waits for them, and re-layouts, copied_route(): expert_mlp(incoming.reshape(-1, MODEL_WIDTH), w_in_local, w_down_local)  7.59 us
  transfers between devices with their start and end apart: 6, of which 4 were waited for; matrix products, arithmetic and copies ran while one was open for 17% of the time, Pallas kernels for 0%

commit v1 on v0

--- a/solution.py
+++ b/solution.py
@@ -14,6 +14,28 @@
 EPSILON = 1e-05
 ROPE_BASE = 150000.0
 GLU_ALPHA = 1.702
+
+
+def in_order(parts, dim):
+    shape = list(parts.shape[1:])
+    shape[dim] *= parts.shape[0]
+    return jnp.moveaxis(parts, 0, dim).reshape(shape)
+
+
+def gather_around(x, axis, dim):
+    count = lax.axis_size(axis)
+    pairs = [(i, (i + 1) % count) for i in range(count)]
+    back = [(b, a) for a, b in pairs]
+    lower, upper = ([], [])
+    for hop in range(count - 1):
+        if hop % 2 == 0:
+            lower.append(lax.ppermute(lower[-1] if lower else x, axis, pairs))
+        else:
+            upper.append(lax.ppermute(upper[-1] if upper else x, axis, back))
+    blocks = jnp.stack([*lower[::-1], x, *upper])
+    shift = lax.axis_index(axis) - len(lower)
+    blocks = blocks[(jnp.arange(count) - shift) % count]
+    return in_order(blocks, dim)
 
 
 def passed_along(array, axis, by):
@@ -152,7 +174,7 @@
     groups = sinks.shape[0] // QUERY_PER_KEY
     normed_input = normalize(tokens, norm_gain_attn).astype(jnp.bfloat16)
     projected_rows = jnp.dot(
-        lax.all_gather(normed_input, "head", axis=0, tiled=True),
+        gather_around(normed_input, "head", 0),
         query_key_value_weight,
         preferred_element_type=jnp.float32,
     ).reshape(tok_dev, groups, QUERY_PER_KEY + 2, HEAD_SIZE)

time: 339 us -> 348 us (1.027)
  waiting for transfers between devices: 196 us -> 183 us
  local copies, waits for them, and re-layouts: 50.4 us -> 60.6 us
  starting transfers between devices: 27.2 us -> 36.2 us
    all_gather x1 -> x0, waiting for transfers between devices: 22.5 us -> none  [per_device(): lax.all_gather(normed_input, 'head', axis=0, tiled=True)]
    unnamed x32 -> x45, local copies, waits for them, and re-layouts: 0.19 us -> 10.8 us
    ppermute x0 -> x7, waiting for transfers between devices: none -> 10.3 us  [the longest x4 10.3 us: gather_around(): lower.append(lax.ppermute(lower[-1] if lower else x, axis, pairs))]
    ppermute x0 -> x7, starting transfers between devices: none -> 8.89 us  [the longest x3 8.86 us: gather_around(): upper.append(lax.ppermute(upper[-1] if upper else x, axis, back))]
  transfers between devices with their start and end apart: 6 -> 12, of which waited for: 4 -> 6; matrix products, arithmetic and copies ran while one was open for 17% -> 20% of each run, Pallas kernels for 0% -> 0%
where the time goes in v1:
time: 348 us; the launch traced here: 347 us
  waiting for transfers between devices  183 us (53%)
  local copies, waits for them, and re-layouts  60.6 us (17%)
  starting transfers between devices  36.2 us (10%)
  matrix products  26.9 us (8%)
  other arithmetic  25.5 us (7%)
  between operations  14.5 us (4%)
    all_to_all x2, waiting for transfers between devices, flat_route(): lax.all_to_all(blocks, ('tok', 'head'), split_axis=0, concat_axis=0, tile...  142 us
    reduce_scatter x1, waiting for transfers between devices, per_device(): lax.psum_scatter(jnp.dot(attended, w_out_attn, preferred_element_type=jnp...  30.9 us
    all_to_all x2, starting transfers between devices, flat_route(): lax.all_to_all(blocks, ('tok', 'head'), split_axis=0, concat_axis=0, tile...  16.4 us
    unnamed x45, local copies, waits for them, and re-layouts  10.8 us
    dot_general x1, matrix products, expert_mlp(): gate_up = jnp.dot(rows_in, w_in_local, preferred_element_type=jnp.float32)  10.8 us
    ppermute x4, waiting for transfers between devices, gather_around(): lower.append(lax.ppermute(lower[-1] if lower else x, axis, pairs))  10.3 us
    ppermute x3, starting transfers between devices, gather_around(): upper.append(lax.ppermute(upper[-1] if upper else x, axis, back))  8.86 us
    reshape x1, local copies, waits for them, and re-layouts, copied_route(): incoming.reshape(-1, MODEL_WIDTH)  8.19 us
  transfers between devices with their start and end apart: 12, of which 6 were waited for; matrix products, arithmetic and copies ran while one was open for 20% of the time, Pallas kernels for 0%

profile of v1, /device:TPU:0, one launch (start us, length us, event | category | flops | bytes accessed | tf_op | source)
XLA Modules:
  0.0 346.7 jit_solution(976185975121111466)
XLA Ops:
  7.2 1.2 fusion.13
  8.5 1.7 fusion.15
  10.2 3.0 collective-permute-start.4
  13.8 6.2 %copy.61 = bf16[2880,640]{0,1:T(8,128)(2,1)} copy(bf16[2880,640]{1,0:T(8,128)(2,1)} %param.15) | data formatting | bytes 7372800 | tf_op args[3]
  21.6 0.9 fusion.22
  22.5 5.3 %collective-permute-done.1 = bf16[32,2880]{1,0:T(8,128)(2,1)S(1)} collective-permute-done((bf16[32,2880]{1,0:T(8,128)(2,1)S(1)}, bf16[32,2880]{1,0:T(8,128)(2,1)S(1)}, u32[]{:S(2)}, u32[]{:S(2)}) %collective-permute-start.1) | collective-permute-done | bytes 184352 | tf_op jit(solution)/shard_map/ppermute | solution.py:32
  27.8 3.0 collective-permute-start.5
  30.7 3.3 collective-permute-done.2
  34.0 1.5 multiply_cosine_fusion
  35.5 3.0 collective-permute-start.6
  38.4 1.8 collective-permute-done.3
  43.0 1.5 bitcast_dynamic-update-slice_fusion.3
  46.6 3.2 gather_fusion
  49.8 3.7 %convolution_bitcast_fusion = f32[256,1,10,64]{0,3,2,1:T(8,128)S(1)} fusion(bf16[256,2880,1]{1,0,2:T(8,128)(2,1)} %bitcast.150, bf16[10,64,2880]{2,1,0:T(8,128)(2,1)} %bitcast.149), kind=kOutput, calls=%fused_computation.20 | convolution fusion | flops 943718400 | bytes 5816320 | tf_op jit(solution)/shard_map/dot_general | solution.py:176
  54.4 4.5 %collective-permute-start.7 = (bf16[128,1,128]{0,2,1:T(8,128)(2,1)}, bf16[128,1,128]{0,2,1:T(8,128)(2,1)}, u32[]{:S(2)}, u32[]{:S(2)}) collective-permute-start(bf16[128,1,128]{0,2,1:T(8,128)(2,1)} %pad_maximum_fusion.3), channel_id=1, source_target_pairs={{0,8},{8,16},{16,24},{24,32},{32,40},{40,48},{48,56},{56,64},{64,7... | collective-permute-start | bytes 98312 | tf_op jit(solution)/shard_map/ppermute | solution.py:44
  58.9 0.8 multiply_subtract_fusion
  60.9 1.8 concatenate.85
  62.7 1.7 copy.67
  64.4 0.8 concatenate.86
  65.2 1.0 copy.68
  66.2 0.8 copy_bitcast_fusion
  67.7 1.5 fusion.6
  70.2 2.2 convolution_convert_fusion.1
  73.1 30.9 %reduce-scatter.2.cloned.1.call-done = bf16[32,2880]{1,0:T(8,128)(2,1)} async-done(((bf16[256,2880]{1,0:T(8,128)(2,1)}), bf16[32,2880]{1,0:T(8,128)(2,1)}) %reduce-scatter.2.cloned.1.call-update) | async-done | bytes 184336 | tf_op jit(solution)/shard_map/reduce_scatter | solution.py:201
  104.1 1.1 multiply_reduce_fusion.1
  105.2 1.0 multiply_convert_fusion
  106.2 1.3 gather_fusion.1
  107.6 1.4 reshape.897
  109.0 1.6 broadcast_select_fusion
  110.6 3.0 broadcast_in_dim.93
  113.6 8.0 %all-to-all-start = ((bf16[128,6,2880]{2,1,0:T(8,128)(2,1)}), bf16[128,6,2880]{2,1,0:T(8,128)(2,1)}, u32[]{:S(2)}, u32[]{:S(2)}) async-start(bf16[128,6,2880]{2,1,0:T(8,128)(2,1)} %bitcast.148), calls=%async_computation.1 | async-start | bytes 12058624 | tf_op jit(solution)/shard_map/all_to_all | solution.py:226
  122.7 1.2 gather_fusion.3
  123.9 70.6 %all-to-all-done = bf16[128,6,2880]{2,1,0:T(8,128)(2,1)} async-done(((bf16[128,6,2880]{2,1,0:T(8,128)(2,1)}), bf16[128,6,2880]{2,1,0:T(8,128)(2,1)}, u32[]{:S(2)}, u32[]{:S(2)}) %all-to-all-start) | async-done | bytes 4423712 | tf_op jit(solution)/shard_map/all_to_all | solution.py:226
  194.6 6.4 %all-to-all-start.2 = ((bf16[16,1,16,1,128]{4,2,3,1,0:T(8,128)(2,1)}), bf16[16,1,16,1,128]{4,2,3,1,0:T(8,128)(2,1)S(1)}, u32[]{:S(2)}, u32[]{:S(2)}) async-start(bf16[16,1,16,1,128]{4,2,3,1,0:T(8,128)(2,1)} %bitcast.49), calls=%async_computation.3 | async-start | bytes 131072 | tf_op jit(solution)/shard_map/all_to_all | solution.py:247
  201.0 8.2 %reshape.878 = bf16[768,2880]{1,0:T(8,128)(2,1)} reshape(bf16[128,6,2880]{2,1,0:T(8,128)(2,1)} %all-to-all-done) | data formatting | bytes 8847360 | tf_op jit(solution)/shard_map/reshape | solution.py:135
  209.1 10.8 %fusion = f32[768,1440]{0,1:T(8,128)S(1)} fusion(bf16[768,2880]{1,0:T(8,128)(2,1)} %reshape.878, bf16[1,2880,1440]{1,2,0:T(8,128)(2,1)} %param.21), kind=kOutput, calls=%fused_computation.6 | convolution fusion | flops 6370099200 | bytes 17141760 | tf_op jit(solution)/shard_map/dot_general | solution.py:121
  220.0 8.1 %convolution_convert_fusion = bf16[768,2880]{0,1:T(8,128)(2,1)} fusion(bf16[1,720,2880]{2,1,0:T(8,128)(2,1)} %param.22, f32[768,1440]{0,1:T(8,128)S(1)} %fusion), kind=kOutput, calls=%fused_computation.8 | convolution fusion | flops 3191685120 | bytes 12994560 | tf_op jit(solution)/shard_map/dot_general | solution.py:127
  228.1 6.5 %copy.73 = bf16[768,2880]{1,0:T(8,128)(2,1)} copy(bf16[768,2880]{0,1:T(8,128)(2,1)} %convolution_convert_fusion) | data formatting | bytes 8847360 | tf_op jit(solution)/shard_map/convert_element_type | solution.py:127
  234.6 7.6 %reshape.879 = bf16[128,6,2880]{2,1,0:T(8,128)(2,1)} reshape(bf16[768,2880]{1,0:T(8,128)(2,1)} %copy.73) | data formatting | bytes 8847360 | tf_op jit(solution)/shard_map/reshape | solution.py:135
  242.2 8.4 %all-to-all-start.1 = ((bf16[128,6,2880]{2,1,0:T(8,128)(2,1)}), bf16[128,6,2880]{2,1,0:T(8,128)(2,1)}, u32[]{:S(2)}, u32[]{:S(2)}) async-start(bf16[128,6,2880]{2,1,0:T(8,128)(2,1)} %reshape.879), calls=%async_computation.2 | async-start | bytes 12058624 | tf_op jit(solution)/shard_map/all_to_all | solution.py:226
  251.4 1.0 scatter_fusion
  252.4 71.2 %all-to-all-done.1 = bf16[128,6,2880]{2,1,0:T(8,128)(2,1)} async-done(((bf16[128,6,2880]{2,1,0:T(8,128)(2,1)}), bf16[128,6,2880]{2,1,0:T(8,128)(2,1)}, u32[]{:S(2)}, u32[]{:S(2)}) %all-to-all-start.1) | async-done | bytes 4423712 | tf_op jit(solution)/shard_map/all_to_all | solution.py:226
  323.6 6.0 %convert_reduce_fusion = f32[32,6,2880]{2,1,0:T(8,128)} fusion(bf16[128,6,2880]{2,1,0:T(8,128)(2,1)} %all-to-all-done.1), kind=kLoop, calls=%fused_computation.5 | loop fusion | flops 3870720 | bytes 6635520 | tf_op jit(solution)/shard_map/reduce_sum | solution.py:139
  329.6 2.0 reshape.882
  331.6 2.3 gather_fusion.2
  333.8 2.9 reshape.905
  336.7 2.4 multiply_reduce_fusion
  339.2 0.7 add_convert_fusion
  (128 shorter events, 13.4 us)
Async XLA Ops:
  7.2 63.0 %copy-start = (bf16[512,2880]{0,1:T(8,128)(2,1)S(1)}, bf16[512,2880]{0,1:T(8,128)(2,1)}, u32[]{:S(2)}) copy-start(bf16[512,2880]{0,1:T(8,128)(2,1)} %param.17) | copy-start | bytes 8847364
  7.2 96.9 %reduce-scatter.2.cloned.1.call-start = ((), (), s32[]{:S(2)}) async-start(), calls=%async_computation.4 | async-start | bytes 1695744 | tf_op jit(solution)/shard_map/reduce_scatter | solution.py:201
  8.5 1.7 copy-start.12
  10.2 11.3 %collective-permute-start = (bf16[32,2880]{1,0:T(8,128)(2,1)}, bf16[32,2880]{1,0:T(8,128)(2,1)S(1)}, u32[]{:S(2)}, u32[]{:S(2)}) collective-permute-start(bf16[32,2880]{1,0:T(8,128)(2,1)} %fusion.15), channel_id=1, source_target_pairs={{0,1},{1,2},{2,3},{3,4},{4,5},{5,6},{6,7},{7,0},{8,9},{9,10},{10,1... | collective-permute-start | bytes 552968 | tf_op jit(solution)/shard_map/ppermute | solution.py:32
  10.2 17.6 %collective-permute-start.4 = (bf16[32,2880]{1,0:T(8,128)(2,1)}, bf16[32,2880]{1,0:T(8,128)(2,1)S(1)}, u32[]{:S(2)}, u32[]{:S(2)}) collective-permute-start(bf16[32,2880]{1,0:T(8,128)(2,1)} %fusion.15), channel_id=1, source_target_pairs={{1,0},{2,1},{3,2},{4,3},{5,4},{6,5},{7,6},{0,7},{9,8},{10,9},{11,1... | collective-permute-start | bytes 552968 | tf_op jit(solution)/shard_map/ppermute | solution.py:34
  13.8 6.2 %copy-start.17 = (s32[4]{0:T(128)S(1)}, s32[4]{0:T(128)}, u32[]{:S(2)}) copy-start(s32[4]{0:T(128)} %param.13) | copy-start | bytes 52
  13.8 7.1 %copy-start.18 = (f32[8]{0:T(128)S(1)}, f32[8]{0:T(128)}, u32[]{:S(2)}) copy-start(f32[8]{0:T(128)} %param.16) | copy-start | bytes 100
  13.8 29.1 %copy-start.2 = (bf16[32,2880]{1,0:T(8,128)(2,1)S(1)}, bf16[32,2880]{1,0:T(8,128)(2,1)}, u32[]{:S(2)}) copy-start(bf16[32,2880]{1,0:T(8,128)(2,1)} %param.12) | copy-start | bytes 552964
  20.2 0.5 copy-start.13
  21.5 6.2 %collective-permute-start.1 = (bf16[32,2880]{1,0:T(8,128)(2,1)S(1)}, bf16[32,2880]{1,0:T(8,128)(2,1)S(1)}, u32[]{:S(2)}, u32[]{:S(2)}) collective-permute-start(bf16[32,2880]{1,0:T(8,128)(2,1)S(1)} %collective-permute-done), channel_id=1, source_target_pairs={{0,1},{1,2},{2,3},{3,4},{4,5},{5,6},{6,7},{7,0},{8,9},{9,10},{10,1... | collective-permute-start | bytes 552968 | tf_op jit(solution)/shard_map/ppermute | solution.py:32
  27.8 6.2 %collective-permute-start.2 = (bf16[32,2880]{1,0:T(8,128)(2,1)S(1)}, bf16[32,2880]{1,0:T(8,128)(2,1)S(1)}, u32[]{:S(2)}, u32[]{:S(2)}) collective-permute-start(bf16[32,2880]{1,0:T(8,128)(2,1)S(1)} %collective-permute-done.1), channel_id=1, source_target_pairs={{0,1},{1,2},{2,3},{3,4},{4,5},{5,6},{6,7},{7,0},{8,9},{9,10},{10,1... | collective-permute-start | bytes 552968 | tf_op jit(solution)/shard_map/ppermute | solution.py:32
  27.8 7.7 %collective-permute-start.5 = (bf16[32,2880]{1,0:T(8,128)(2,1)S(1)}, bf16[32,2880]{1,0:T(8,128)(2,1)S(1)}, u32[]{:S(2)}, u32[]{:S(2)}) collective-permute-start(bf16[32,2880]{1,0:T(8,128)(2,1)S(1)} %collective-permute-done.4), channel_id=1, source_target_pairs={{1,0},{2,1},{3,2},{4,3},{5,4},{6,5},{7,6},{0,7},{9,8},{10,9},{11,1... | collective-permute-start | bytes 552968 | tf_op jit(solution)/shard_map/ppermute | solution.py:34
  34.0 6.2 %collective-permute-start.3 = (bf16[32,2880]{1,0:T(8,128)(2,1)S(1)}, bf16[32,2880]{1,0:T(8,128)(2,1)S(1)}, u32[]{:S(2)}, u32[]{:S(2)}) collective-permute-start(bf16[32,2880]{1,0:T(8,128)(2,1)S(1)} %collective-permute-done.2), channel_id=1, source_target_pairs={{0,1},{1,2},{2,3},{3,4},{4,5},{5,6},{6,7},{7,0},{8,9},{9,10},{10,1... | collective-permute-start | bytes 552968 | tf_op jit(solution)/shard_map/ppermute | solution.py:32
  35.5 10.4 %collective-permute-start.6 = (bf16[32,2880]{1,0:T(8,128)(2,1)S(1)}, bf16[32,2880]{1,0:T(8,128)(2,1)S(1)}, u32[]{:S(2)}, u32[]{:S(2)}) collective-permute-start(bf16[32,2880]{1,0:T(8,128)(2,1)S(1)} %collective-permute-done.5), channel_id=1, source_target_pairs={{1,0},{2,1},{3,2},{4,3},{5,4},{6,5},{7,6},{0,7},{9,8},{10,9},{11,1... | collective-permute-start | bytes 552968 | tf_op jit(solution)/shard_map/ppermute | solution.py:34
  49.8 3.8 %copy-start.11 = (f32[32]{0:T(128)S(1)}, f32[32]{0:T(128)}, u32[]{:S(2)}) copy-start(f32[32]{0:T(128)} %multiply_exponential_fusion) | copy-start | bytes 388
  49.8 9.1 %copy-start.6 = (f32[256,32]{0,1:T(8,128)S(1)}, f32[256,32]{0,1:T(8,128)}, u32[]{:S(2)}) copy-start(f32[256,32]{0,1:T(8,128)} %get-tuple-element.13) | copy-start | bytes 98308
  54.4 11.8 %collective-permute-start.7 = (bf16[128,1,128]{0,2,1:T(8,128)(2,1)}, bf16[128,1,128]{0,2,1:T(8,128)(2,1)}, u32[]{:S(2)}, u32[]{:S(2)}) collective-permute-start(bf16[128,1,128]{0,2,1:T(8,128)(2,1)} %pad_maximum_fusion.3), channel_id=1, source_target_pairs={{0,8},{8,16},{16,24},{24,32},{32,40},{40,48},{48,56},{56,64},{64,7... | collective-permute-start | bytes 98312 | tf_op jit(solution)/shard_map/ppermute | solution.py:44
  60.9 6.1 %copy-start.7 = (bf16[2,128,1,64]{1,3,0,2:T(8,128)(2,1)S(1)}, bf16[2,128,1,64]{1,3,0,2:T(8,128)(2,1)}, u32[]{:S(2)}) copy-start(bf16[2,128,1,64]{1,3,0,2:T(8,128)(2,1)} %copy.65) | copy-start | bytes 98308
  64.4 4.9 %copy-start.16 = (f32[8]{0:T(128)S(1)}, f32[8]{0:T(128)}, u32[]{:S(2)}) copy-start(f32[8]{0:T(128)} %exp.30) | copy-start | bytes 100
  65.2 4.1 %copy-start.4 = (pred[2,128,256]{1,2,0:T(8,128)(4,1)S(1)}, pred[2,128,256]{1,2,0:T(8,128)(4,1)}, u32[]{:S(2)}) copy-start(pred[2,128,256]{1,2,0:T(8,128)(4,1)} %fusion.22) | copy-start | bytes 196612
  70.1 2.3 copy-start.14
  70.1 2.4 copy-start.8
  72.4 32.8 %copy-start.9 = (f32[2880]{0:T(1024)S(1)}, f32[2880]{0:T(1024)}, u32[]{:S(2)}) copy-start(f32[2880]{0:T(1024)} %param.18) | copy-start | bytes 34564
  113.6 8.0 %copy-start.10 = (s32[256]{0:T(256)S(1)}, s32[256]{0:T(256)}, u32[]{:S(2)}) copy-start(s32[256]{0:T(256)} %param.23) | copy-start | bytes 3076
  113.6 81.0 %all-to-all-start = ((bf16[128,6,2880]{2,1,0:T(8,128)(2,1)}), bf16[128,6,2880]{2,1,0:T(8,128)(2,1)}, u32[]{:S(2)}, u32[]{:S(2)}) async-start(bf16[128,6,2880]{2,1,0:T(8,128)(2,1)} %bitcast.148), calls=%async_computation.1 | async-start | bytes 12058624 | tf_op jit(solution)/shard_map/all_to_all | solution.py:226
  194.6 47.6 %all-to-all-start.2 = ((bf16[16,1,16,1,128]{4,2,3,1,0:T(8,128)(2,1)}), bf16[16,1,16,1,128]{4,2,3,1,0:T(8,128)(2,1)S(1)}, u32[]{:S(2)}, u32[]{:S(2)}) async-start(bf16[16,1,16,1,128]{4,2,3,1,0:T(8,128)(2,1)} %bitcast.49), calls=%async_computation.3 | async-start | bytes 131072 | tf_op jit(solution)/shard_map/all_to_all | solution.py:247
  242.2 8.9 %copy-start.15 = (f32[32,4]{0,1:T(4,128)S(1)}, f32[32,4]{0,1:T(4,128)}, u32[]{:S(2)}) copy-start(f32[32,4]{0,1:T(4,128)} %param.20) | copy-start | bytes 1540
  242.2 81.4 %all-to-all-start.1 = ((bf16[128,6,2880]{2,1,0:T(8,128)(2,1)}), bf16[128,6,2880]{2,1,0:T(8,128)(2,1)}, u32[]{:S(2)}, u32[]{:S(2)}) async-start(bf16[128,6,2880]{2,1,0:T(8,128)(2,1)} %reshape.879), calls=%async_computation.2 | async-start | bytes 12058624 | tf_op jit(solution)/shard_map/all_to_all | solution.py:226
  252.4 77.2 %copy-start.5 = (bf16[16,16,128]{2,1,0:T(8,128)(2,1)}, bf16[16,16,128]{2,1,0:T(8,128)(2,1)S(1)}, u32[]{:S(2)}) copy-start(bf16[16,16,128]{2,1,0:T(8,128)(2,1)S(1)} %scatter_fusion) | copy-start | bytes 196612
  333.8 5.3 %copy-start.3 = (bf16[32,2880]{1,0:T(8,128)(2,1)S(1)}, bf16[32,2880]{1,0:T(8,128)(2,1)}, u32[]{:S(2)}) copy-start(bf16[32,2880]{1,0:T(8,128)(2,1)} %reduce-scatter.2.cloned.1.call-done) | copy-start | bytes 552964
  333.8 6.1 %copy-start.1 = (bf16[512,2880]{0,1:T(8,128)(2,1)S(1)}, bf16[512,2880]{0,1:T(8,128)(2,1)}, u32[]{:S(2)}) copy-start(bf16[512,2880]{0,1:T(8,128)(2,1)} %param.17) | copy-start | bytes 8847364
Sparse Core Ops, SparseCore 0:
  72.5 31.5 reduce-scatter.1
